TPU v7x, 32 devices: a whole 2x2x4 slice. The times are simulated.
32 devices in a mesh: gx: 4 (over x, core), gy: 8 (over z, y).
Axes of the slice: x: 2, y: 2, z: 4, core: 2. Of those that a mesh axis runs over, the one named last changes fastest.
Arguments:
- queries: bfloat16 [256, 2560], P('gx'), may hold values from -8 to 8
- token_key_value: bfloat16 [256, 1024], P('gx'), may hold values from -6 to 6
- group_cached_keys: bfloat16 [4, 32768, 512], P('gx', 'gy'), may hold values from -8 to 8
- group_cached_values: bfloat16 [4, 32768, 512], P('gx', 'gy'), may hold values from -6 to 6
- owners: int32 [4, 32768], P('gx', 'gy'), may hold values from 0 to 63, never falling along the last dimension, each value on 1 to 16384 neighbouring positions
- out_weight: bfloat16 [2560, 2560], P(None, 'gy'), may hold values from -0.125 to 0.125
- residual: bfloat16 [256, 2560], P('gx', 'gy'), may hold values from -6 to 6
- norm_gain: bfloat16 [2560], P('gy'), may hold values from 0.099609375 to 1.8984375
- expert_ids: int32 [256, 6], replicated, may hold values from 0 to 63, all different within a row; in each aligned block of 64 rows (0 to 63, 64 to 127, ...) at most 12 rows name the same one
- gate_logits: float32 [256, 6], replicated, may hold values from -0.5 to 0.5
- w_gate_up: bfloat16 [64, 2560, 3072], P('gx', 'gy'), may hold values from -0.125 to 0.125
- w_down: bfloat16 [64, 1536, 2560], P('gx', None, 'gy'), may hold values from -0.15625 to 0.15625
Outputs:
- layer_out: float32 [256, 2560], P('gx', 'gy')
Inputs may be any that keep to these rules, and one draw needn't show every extreme that they name: `owners`: each request's positions form one run; every request owns at least one position and at most 16384, and some request owns exactly 16384. `expert_ids`: within each group of 64 requests no expert is named by more than 12 requests, a bound that some block reaches.
All inputs are finite; a program needn't handle non-finite values.
Results may differ from a plain program's by a relative error of at most 0.0075.
Values may be sent and summed in bfloat16 or wider, within the bound.
No kernel may reach another device: no remote copies, remote signals or barrier semaphores. Data moves between devices by JAX's collectives and lax.ppermute only.
A program may use at most 192 MiB of HBM per device.

v0:
```python
import jax
import jax.numpy as jnp
from jax import lax
from jax.sharding import PartitionSpec as P

D = 2560
QUERY_HEADS = 20
KEY_VALUE_HEADS = 4
HEAD_SIZE = 128
E = 64
TOPK = 6
CAPS = 12
minimal_score = -1e30
norm_epsilon = 1e-05


def merged(part, axis, combine):
    gathered = jax.tree.map(lambda a: lax.all_gather(a, axis), part)

    def take(source):
        return jax.tree.map(lambda a: lax.dynamic_index_in_dim(a, source, 0, False), gathered)

    return lax.fori_loop(
        1, lax.axis_size(axis), lambda source, state: combine(state, take(source)), take(0)
    )


def merge_partial(earlier_part, later_part):
    max_one, den_one, acc_one = earlier_part
    max_two, den_two, acc_two = later_part
    peak = jnp.maximum(max_one, max_two)
    scale_one = jnp.exp(max_one - peak)
    scale_two = jnp.exp(max_two - peak)
    return (
        peak,
        den_one * scale_one + den_two * scale_two,
        acc_one * scale_one[..., None] + acc_two * scale_two[..., None],
    )


def slot_ranks(flat_ids, num_experts):
    onehot = (flat_ids[..., None] == lax.iota(jnp.int32, num_experts)).astype(jnp.int32)
    earlier = jnp.cumsum(onehot, axis=-2) - onehot
    return jnp.sum(earlier * onehot, axis=-1)


def attend_local(queries, group_cached_keys, group_cached_values, owners):
    request_rows = queries.shape[0]
    query_heads_per_group = QUERY_HEADS // KEY_VALUE_HEADS
    positions = group_cached_keys.shape[0]
    block_length = min(positions, 512)
    block_count = positions // block_length
    key_block_list = group_cached_keys.reshape(
        block_count, block_length, KEY_VALUE_HEADS, HEAD_SIZE
    )
    value_block_list = group_cached_values.reshape(
        block_count, block_length, KEY_VALUE_HEADS, HEAD_SIZE
    )
    owner_blocks = owners.reshape(block_count, block_length)
    scaling = HEAD_SIZE ** (-0.5)
    request_ids = lax.iota(jnp.int32, request_rows)

    def visit_block(state_in, inputs):
        run_max, run_den, run_acc = state_in
        key_block, value_block, owning_block = inputs
        picked_experts = queries[owning_block].reshape(
            block_length, KEY_VALUE_HEADS, query_heads_per_group, HEAD_SIZE
        )
        scores = (
            jnp.einsum(
                "tkgd,tkd->tkg", picked_experts, key_block, preferred_element_type=jnp.float32
            )
            * scaling
        )
        member = owning_block[:, None] == request_ids[None, :]
        block_max = jnp.max(
            jnp.where(member[:, :, None, None], scores[:, None], minimal_score), axis=0
        )
        new_max = jnp.maximum(run_max, block_max)
        prob_block = jnp.exp(scores - new_max[owning_block]).astype(jnp.bfloat16)
        spread = jnp.where(
            member[:, :, None, None], prob_block[:, None], jnp.zeros((), jnp.bfloat16)
        )
        rescale = jnp.exp(run_max - new_max)
        run_den = run_den * rescale + jnp.sum(spread.astype(jnp.float32), axis=0)
        run_acc = run_acc * rescale[..., None] + jnp.einsum(
            "trkg,tkd->rkgd", spread, value_block, preferred_element_type=jnp.float32
        )
        return ((new_max, run_den, run_acc), None)

    initial = (
        jnp.full(
            (request_rows, KEY_VALUE_HEADS, query_heads_per_group), minimal_score, jnp.float32
        ),
        jnp.zeros((request_rows, KEY_VALUE_HEADS, query_heads_per_group), jnp.float32),
        jnp.zeros((request_rows, KEY_VALUE_HEADS, query_heads_per_group, HEAD_SIZE), jnp.float32),
    )
    return lax.scan(visit_block, initial, (key_block_list, value_block_list, owner_blocks))[0]


def expert_block(tokens, w_gate_up, w_down):
    hidden_units = w_down.shape[1]
    gate_up = jnp.einsum("sekd,edf->sekf", tokens, w_gate_up, preferred_element_type=jnp.float32)
    gate_up = lax.psum(gate_up, "gy")
    active = (jax.nn.silu(gate_up[..., :hidden_units]) * gate_up[..., hidden_units:]).astype(
        jnp.bfloat16
    )
    return jnp.einsum("sekf,efd->sekd", active, w_down, preferred_element_type=jnp.float32).astype(
        jnp.bfloat16
    )


def shards(
    queries,
    token_key_value,
    group_cached_keys,
    group_cached_values,
    owners,
    out_weight,
    residual,
    norm_gain,
    expert_ids,
    gate_logits,
    w_gate_up,
    w_down,
):
    request_rows = queries.shape[0]
    query_heads_per_group = QUERY_HEADS // KEY_VALUE_HEADS
    key_value_width = token_key_value.shape[1] // 2
    scaling = HEAD_SIZE ** (-0.5)
    run_max, run_den, run_acc = attend_local(
        queries, group_cached_keys[0], group_cached_values[0], owners[0]
    )
    query_head_rows = queries.reshape(
        request_rows, KEY_VALUE_HEADS, query_heads_per_group, HEAD_SIZE
    )
    appended_keys = token_key_value[:, :key_value_width].reshape(
        request_rows, KEY_VALUE_HEADS, HEAD_SIZE
    )
    appended_values = token_key_value[:, key_value_width:]
    own_score = (
        jnp.einsum(
            "rkgd,rkd->rkg", query_head_rows, appended_keys, preferred_element_type=jnp.float32
        )
        * scaling
    )
    run_max, run_den, run_acc = merged((run_max, run_den, run_acc), "gy", merge_partial)
    peak = jnp.maximum(run_max, own_score)
    rescale = jnp.exp(run_max - peak)
    own_prob = lax.optimization_barrier(jnp.exp(own_score - peak).astype(jnp.bfloat16)).astype(
        jnp.float32
    )
    denominator = run_den * rescale + own_prob
    incoming_values = appended_values.astype(jnp.float32).reshape(
        request_rows, KEY_VALUE_HEADS, 1, HEAD_SIZE
    )
    numerator = run_acc * rescale[..., None] + own_prob[..., None] * incoming_values
    attention = (
        (numerator / denominator[..., None])
        .astype(jnp.bfloat16)
        .reshape(request_rows, QUERY_HEADS * HEAD_SIZE)
    )
    projected = jnp.dot(attention, out_weight, preferred_element_type=jnp.float32)
    hidden = (residual.astype(jnp.float32) + projected).astype(jnp.bfloat16)
    hidden_f = hidden.astype(jnp.float32)
    squares = lax.psum(jnp.sum(hidden_f * hidden_f, axis=1), "gy")
    inv_rms = lax.rsqrt(squares / D + norm_epsilon)
    normed = (hidden_f * inv_rms[:, None] * norm_gain.astype(jnp.float32)[None, :]).astype(
        jnp.bfloat16
    )
    mixing = jax.nn.softmax(gate_logits, axis=-1)
    num_gx = lax.axis_size("gx")
    group_index = lax.axis_index("gx")
    per_row = w_gate_up.shape[0]
    columns_here = normed.shape[1]
    my_ids = lax.dynamic_slice_in_dim(
        expert_ids, group_index * request_rows, request_rows, 0
    ).reshape(-1)
    my_mix = lax.dynamic_slice_in_dim(mixing, group_index * request_rows, request_rows, 0)
    places = my_ids * CAPS + slot_ranks(my_ids, E)
    outgoing = (
        jnp.zeros((E * CAPS, columns_here), jnp.bfloat16)
        .at[places]
        .set(jnp.repeat(normed, TOPK, axis=0))
    )
    returned = lax.all_to_all(
        expert_block(
            lax.all_to_all(
                outgoing.reshape(num_gx, per_row, CAPS, columns_here),
                "gx",
                split_axis=0,
                concat_axis=0,
                tiled=True,
            ),
            w_gate_up,
            w_down,
        ),
        "gx",
        split_axis=0,
        concat_axis=0,
        tiled=True,
    )
    picked = (
        returned.reshape(E * CAPS, columns_here)[places]
        .astype(jnp.float32)
        .reshape(request_rows, TOPK, columns_here)
    )
    routed = jnp.sum(my_mix[..., None] * picked, axis=1)
    return hidden_f + routed


def solution(mesh):
    placed = (
        P("gx", None),
        P("gx", None),
        P("gx", "gy", None),
        P("gx", "gy", None),
        P("gx", "gy"),
        P(None, "gy"),
        P("gx", "gy"),
        P("gy"),
        P(),
        P(),
        P("gx", "gy", None),
        P("gx", None, "gy"),
    )
    return jax.shard_map(
        shards, mesh=mesh, in_specs=placed, out_specs=P("gx", "gy"), check_vma=False
    )
```

profile of v0, /device:TPU:0, one launch (start us, length us, event | category | flops | bytes accessed | tf_op | source)
XLA Modules:
  0.0 817.4 jit_solution(4890092526414652480)
XLA Ops:
  6.5 7.0 reshape.208
  13.6 7.0 reshape_squeeze.10
  22.4 178.0 %while.35 = (s32[]{:T(128)}, f32[64,4,5]{2,1,0:T(4,128)S(1)}, f32[64,4,5]{2,1,0:T(4,128)S(1)}, f32[64,4,5,128]{3,0,2,1:T(8,128)}, s32[8,512]{1,0:T(8,128)}, /*in...) while((s32[]{:T(128)}, f32[64,4,5]{2,1,0:T(4,128)S(1)}, ...), condition=%wide.region_3.4_spmd.clone, body=%wide.region_0.3_spmd.clone.sunk | while | flops 176462592 | bytes 21555320 | solution.py:98
  23.1 3.6 gather_fusion
  26.7 4.5 copy.169
  31.2 2.1 bitcast_convert_fusion.2
  34.9 2.3 multiply_reduce_fusion.4
  37.8 2.1 gather_fusion.1
  44.4 3.6 gather_fusion
  48.0 4.5 copy.169
  52.5 2.1 bitcast_convert_fusion.2
  56.2 2.3 multiply_reduce_fusion.4
  59.1 2.1 gather_fusion.1
  63.6 2.4 fusion.70
  66.8 3.6 gather_fusion
  70.4 4.5 copy.169
  74.9 2.1 bitcast_convert_fusion.2
  78.6 2.3 multiply_reduce_fusion.4
  81.5 2.1 gather_fusion.1
  86.0 2.4 fusion.70
  89.2 3.6 gather_fusion
  92.8 4.5 copy.169
  97.3 2.1 bitcast_convert_fusion.2
  101.0 2.3 multiply_reduce_fusion.4
  103.9 2.1 gather_fusion.1
  108.4 2.4 fusion.70
  111.6 3.6 gather_fusion
  115.2 4.5 copy.169
  119.7 2.1 bitcast_convert_fusion.2
  123.4 2.3 multiply_reduce_fusion.4
  126.3 2.1 gather_fusion.1
  130.8 2.4 fusion.70
  134.0 3.6 gather_fusion
  137.6 4.5 copy.169
  142.1 2.1 bitcast_convert_fusion.2
  145.8 2.3 multiply_reduce_fusion.4
  148.7 2.1 gather_fusion.1
  153.2 2.4 fusion.70
  156.4 3.6 gather_fusion
  160.0 4.5 copy.169
  164.5 2.1 bitcast_convert_fusion.2
  168.1 2.3 multiply_reduce_fusion.4
  171.1 2.1 gather_fusion.1
  175.6 2.4 fusion.70
  178.8 3.6 gather_fusion
  182.4 4.5 copy.169
  186.8 2.1 bitcast_convert_fusion.2
  190.5 2.3 multiply_reduce_fusion.4
  193.5 2.1 gather_fusion.1
  198.0 2.4 fusion.70
  202.2 38.6 %all-gather = f32[512,4,5]{2,1,0:T(4,128)S(1)} all-gather(f32[64,4,5]{2,1,0:T(4,128)S(1)} %get-tuple-element.232), channel_id=2, replica_groups=mesh['gx'=4,'gy'=8] {'gy'}, dimensions={0}, use_global_device_ids=true | all-gather | bytes 46080 | tf_op jit(solution)/shard_map/all_gather | solution.py:18
  240.9 35.2 %all-gather.1 = f32[512,4,5]{2,1,0:T(4,128)S(1)} all-gather(f32[64,4,5]{2,1,0:T(4,128)S(1)} %get-tuple-element.233), channel_id=3, replica_groups=mesh['gx'=4,'gy'=8] {'gy'}, dimensions={0}, use_global_device_ids=true | all-gather | bytes 46080 | tf_op jit(solution)/shard_map/all_gather | solution.py:18
  282.6 27.2 %all-gather.5.cloned.1.call-done = f32[512,4,5,128]{3,0,2,1:T(8,128)} async-done(((f32[64,4,5,128]{3,0,2,1:T(8,128)}), f32[512,4,5,128]{3,0,2,1:T(8,128)}) %all-gather.5.cloned.1.call-update) | async-done | bytes 5242896 | tf_op jit(solution)/shard_map/all_gather | solution.py:18
  311.4 20.6 %while.34 = (s32[]{:T(128)}, f32[64,4,5]{0,1,2:T(4,128)S(1)}, f32[64,4,5]{0,1,2:T(4,128)S(1)}, f32[64,4,5,128]{3,2,1,0:T(8,128)S(1)}, f32[8,64,4,5]{1,2,3,0:T(4,...) while((s32[]{:T(128)}, f32[64,4,5]{0,1,2:T(4,128)S(1)}, ...), condition=%wide.region_5.6_spmd, body=%wide.region_4.5_spmd.sunk | while | flops 499205 | bytes 3348631 | solution.py:23
  333.7 1.9 divide_convert_fusion
  336.7 19.3 %psum.14 = f32[64]{0:T(128)S(1)} all-reduce(f32[64]{0:T(128)S(1)} %get-tuple-element.365), channel_id=1, replica_groups=mesh['gx'=4,'gy'=8] {'gy'}, use_global_device_ids=true, to_apply=%region_12.13 | all-reduce | flops 64 | bytes 512 | tf_op jit(solution)/shard_map/psum | solution.py:166
  356.3 2.1 scatter_custom_fusion
  358.7 12.1 %all_to_all.10 = bf16[4,16,12,320]{3,1,2,0:T(8,128)(2,1)S(1)} all-to-all(bf16[4,16,12,320]{3,1,2,0:T(8,128)(2,1)S(1)} %copy.108), channel_id=1, replica_groups=mesh['gx'=4,'gy'=8] {'gx'}, dimensions={0} | all-to-all | bytes 983040 | tf_op jit(solution)/shard_map/all_to_all | solution.py:188
  370.8 16.6 %fusion.23 = f32[4,16,12,3072]{3,2,0,1:T(8,128)} fusion(bf16[16,320,3072]{2,1,0:T(8,128)(2,1)} %param.26, bf16[4,16,12,320]{3,1,2,0:T(8,128)(2,1)S(1)} %all_to_all.10), kind=kOutput, calls=%fused_computation.44 | convolution fusion | flops 1509949440 | bytes 41385984 | tf_op jit(solution)/shard_map/sekd,edf->sekf/dot_general | solution.py:103
  388.2 393.0 %all-reduce.2.cloned.1.call-done = f32[4,16,12,3072]{3,2,0,1:T(8,128)} async-done(((f32[4,16,12,3072]{3,2,0,1:T(8,128)}), f32[4,16,12,3072]{3,2,0,1:T(8,128)}) %all-reduce.2.cloned.1.call-update) | async-done | bytes 9437200 | tf_op jit(solution)/shard_map/psum | solution.py:104
  781.2 11.6 %fusion.34 = bf16[4,16,12,320]{3,2,0,1:T(8,128)(2,1)S(1)} fusion(bf16[16,1536,320]{1,2,0:T(8,128)(2,1)} %param.27, f32[4,16,12,3072]{3,2,0,1:T(8,128)} %all-reduce.2.cloned.1.call-done), kind=kOutput, calls=%fused_computation.49 | convolution fusion | flops 762298368 | bytes 25657344 | tf_op jit(solution)/shard_map/sekf,efd->sekd/dot_general | solution.py:108
  793.9 3.5 all-to-all-start.1
  797.7 9.2 %all-to-all-done.1 = bf16[4,16,12,320]{3,1,2,0:T(8,128)(2,1)S(1)} async-done(((bf16[4,16,12,320]{3,1,2,0:T(8,128)(2,1)}), bf16[4,16,12,320]{3,1,2,0:T(8,128)(2,1)S(1)}, u32[]{:S(2)}, u32[]{:S(2)}) %all-to-all-start.1) | async-done | bytes 491552 | tf_op jit(solution)/shard_map/all_to_all | solution.py:186
  807.4 2.1 gather_fusion.2
  (260 shorter events, 82.1 us)
Async XLA Ops:
  6.5 329.4 %copy-start = (bf16[2560,320]{0,1:T(8,128)(2,1)S(1)}, bf16[2560,320]{0,1:T(8,128)(2,1)}, u32[]{:S(2)}) copy-start(bf16[2560,320]{0,1:T(8,128)(2,1)} %param.21) | copy-start | bytes 4915204
  6.5 303.3 %all-gather.5.cloned.1.call-start = ((), (), s32[]{:S(2)}) async-start(), calls=%async_computation.3 | async-start | bytes 5898240 | tf_op jit(solution)/shard_map/all_gather | solution.py:18
  13.6 7.5 copy-start.6
  13.6 8.8 %copy-start.1 = (bf16[64,2560]{1,0:T(8,128)(2,1)S(1)}, bf16[64,2560]{1,0:T(8,128)(2,1)}, u32[]{:S(2)}) copy-start(bf16[64,2560]{1,0:T(8,128)(2,1)} %param.16) | copy-start | bytes 983044
  22.4 179.4 %copy-start.7 = (s32[256,6]{0,1:T(8,128)S(1)}, s32[256,6]{0,1:T(8,128)}, u32[]{:S(2)}) copy-start(s32[256,6]{0,1:T(8,128)} %param.24) | copy-start | bytes 18436
  200.4 78.9 %copy-start.3 = (bf16[64,1024]{1,0:T(8,128)(2,1)S(1)}, bf16[64,1024]{1,0:T(8,128)(2,1)}, u32[]{:S(2)}) copy-start(bf16[64,1024]{1,0:T(8,128)(2,1)} %param.17) | copy-start | bytes 393220
  200.5 80.5 %copy-start.8 = (bf16[320]{0:T(512)(128)(2,1)S(1)}, bf16[320]{0:T(512)(128)(2,1)}, u32[]{:S(2)}) copy-start(bf16[320]{0:T(512)(128)(2,1)} %param.23) | copy-start | bytes 1924
  200.5 580.7 %all-reduce.2.cloned.1.call-start = ((), (), s32[]{:S(2)}) async-start(), calls=%async_computation.2 | async-start | bytes 25165824 | tf_op jit(solution)/shard_map/psum | solution.py:104
  276.2 1.0 copy-start.2
  311.4 24.6 %copy-start.4 = (bf16[64,320]{1,0:T(8,128)(2,1)S(1)}, bf16[64,320]{1,0:T(8,128)(2,1)}, u32[]{:S(2)}) copy-start(bf16[64,320]{1,0:T(8,128)(2,1)} %param.22) | copy-start | bytes 122884
  387.4 0.7 copy-start.5
  793.9 13.0 %all-to-all-start.1 = ((bf16[4,16,12,320]{3,1,2,0:T(8,128)(2,1)}), bf16[4,16,12,320]{3,1,2,0:T(8,128)(2,1)S(1)}, u32[]{:S(2)}, u32[]{:S(2)}) async-start(bf16[4,16,12,320]{3,1,2,0:T(8,128)(2,1)} %copy.110), calls=%async_computation.1 | async-start | bytes 1179648 | tf_op jit(solution)/shard_map/all_to_all | solution.py:186
Sparse Core Ops, SparseCore 0:
  200.6 109.1 all-gather.4
  387.6 393.5 all-reduce.1
where the time goes:
time: 821 us; the launch traced here: 817 us
  waiting for transfers between devices  429 us (52%)
  local copies, waits for them, and re-layouts  151 us (18%)
  blocking collectives  105 us (13%)
  other arithmetic  64.6 us (8%)
  matrix products  48.9 us (6%)
  between operations  13.7 us (2%)
    psum x1, waiting for transfers between devices, expert_block(): gate_up = lax.psum(gate_up, 'gy')  393 us
    all_gather x2, blocking collectives, merged(): gathered = jax.tree.map(lambda a: lax.all_gather(a, axis), part)  73.9 us
    while x24, local copies, waits for them, and re-layouts  48.4 us
    while x16, other arithmetic  35.7 us
    gather x8, local copies, waits for them, and re-layouts, visit_block(): queries[owning_block]  28.5 us
    all_gather x1, waiting for transfers between devices, merged(): gathered = jax.tree.map(lambda a: lax.all_gather(a, axis), part)  27.2 us
    gather x16, local copies, waits for them, and re-layouts, visit_block(): prob_block = jnp.exp(scores - new_max[owning_block]).astype(jnp.bfloat16)  19.4 us
    psum x1, blocking collectives, shards(): squares = lax.psum(jnp.sum(hidden_f * hidden_f, axis=1), 'gy')  19.3 us
  transfers between devices with their start and end apart: 3, of which 3 were waited for; matrix products, arithmetic and copies ran while one was open for 1% of the time, Pallas kernels for 0%

commit v1 on v0

--- a/solution.py
+++ b/solution.py
@@ -101,7 +101,7 @@
 def expert_block(tokens, w_gate_up, w_down):
     hidden_units = w_down.shape[1]
     gate_up = jnp.einsum("sekd,edf->sekf", tokens, w_gate_up, preferred_element_type=jnp.float32)
-    gate_up = lax.psum(gate_up, "gy")
+    gate_up = lax.all_gather(gate_up, "gy").sum(axis=0)
     active = (jax.nn.silu(gate_up[..., :hidden_units]) * gate_up[..., hidden_units:]).astype(
         jnp.bfloat16
     )

time: 821 us -> 2360 us (2.87)
  waiting for transfers between devices: 429 us -> 1930 us
  other arithmetic: 64.6 us -> 101 us
    all_gather x0 -> x1, waiting for transfers between devices: none -> 1890 us  [expert_block(): gate_up = lax.all_gather(gate_up, 'gy').sum(axis=0)]
    psum x1 -> x0, waiting for transfers between devices: 393 us -> none  [expert_block(): gate_up = lax.psum(gate_up, 'gy')]
    reduce_sum x0 -> x1, other arithmetic: none -> 36.1 us  [expert_block(): gate_up = lax.all_gather(gate_up, 'gy').sum(axis=0)]
  transfers between devices with their start and end apart: 3 -> 3, of which waited for: 3 -> 3; matrix products, arithmetic and copies ran while one was open for 1% -> 0% of each run, Pallas kernels for 0% -> 0%
where the time goes in v1:
time: 2360 us; the launch traced here: 2350 us
  waiting for transfers between devices  1930 us (82%)
  local copies, waits for them, and re-layouts  151 us (6%)
  blocking collectives  105 us (4%)
  other arithmetic  101 us (4%)
  matrix products  48.9 us (2%)
    all_gather x1, waiting for transfers between devices, expert_block(): gate_up = lax.all_gather(gate_up, 'gy').sum(axis=0)  1890 us
    all_gather x2, blocking collectives, merged(): gathered = jax.tree.map(lambda a: lax.all_gather(a, axis), part)  73.9 us
    while x24, local copies, waits for them, and re-layouts  48.4 us
  transfers between devices with their start and end apart: 3, of which 3 were waited for; matrix products, arithmetic and copies ran while one was open for 0% of the time, Pallas kernels for 0%

profile of v1, /device:TPU:0, one launch (start us, length us, event | category | flops | bytes accessed | tf_op | source)
XLA Modules:
  0.0 2352.2 jit_solution(11346307846546142163)
XLA Ops:
  6.5 7.0 reshape.209
  13.6 7.0 reshape_squeeze.10
  22.4 178.0 %while.35 = (s32[]{:T(128)}, f32[64,4,5]{2,1,0:T(4,128)S(1)}, f32[64,4,5]{2,1,0:T(4,128)S(1)}, f32[64,4,5,128]{3,0,2,1:T(8,128)}, s32[8,512]{1,0:T(8,128)}, /*in...) while((s32[]{:T(128)}, f32[64,4,5]{2,1,0:T(4,128)S(1)}, ...), condition=%wide.region_3.4_spmd.clone, body=%wide.region_0.3_spmd.clone.sunk | while | flops 176462592 | bytes 21555320 | solution.py:98
  23.1 3.6 gather_fusion
  26.7 4.5 copy.169
  31.2 2.1 bitcast_convert_fusion.2
  34.9 2.3 multiply_reduce_fusion.4
  37.8 2.1 gather_fusion.1
  44.4 3.6 gather_fusion
  48.0 4.5 copy.169
  52.5 2.1 bitcast_convert_fusion.2
  56.2 2.3 multiply_reduce_fusion.4
  59.1 2.1 gather_fusion.1
  63.6 2.4 fusion.70
  66.8 3.6 gather_fusion
  70.4 4.5 copy.169
  74.9 2.1 bitcast_convert_fusion.2
  78.6 2.3 multiply_reduce_fusion.4
  81.5 2.1 gather_fusion.1
  86.0 2.4 fusion.70
  89.2 3.6 gather_fusion
  92.8 4.5 copy.169
  97.3 2.1 bitcast_convert_fusion.2
  101.0 2.3 multiply_reduce_fusion.4
  103.9 2.1 gather_fusion.1
  108.4 2.4 fusion.70
  111.6 3.6 gather_fusion
  115.2 4.5 copy.169
  119.7 2.1 bitcast_convert_fusion.2
  123.4 2.3 multiply_reduce_fusion.4
  126.3 2.1 gather_fusion.1
  130.8 2.4 fusion.70
  134.0 3.6 gather_fusion
  137.6 4.5 copy.169
  142.1 2.1 bitcast_convert_fusion.2
  145.8 2.3 multiply_reduce_fusion.4
  148.7 2.1 gather_fusion.1
  153.2 2.4 fusion.70
  156.4 3.6 gather_fusion
  160.0 4.5 copy.169
  164.5 2.1 bitcast_convert_fusion.2
  168.1 2.3 multiply_reduce_fusion.4
  171.1 2.1 gather_fusion.1
  175.6 2.4 fusion.70
  178.8 3.6 gather_fusion
  182.4 4.5 copy.169
  186.8 2.1 bitcast_convert_fusion.2
  190.5 2.3 multiply_reduce_fusion.4
  193.5 2.1 gather_fusion.1
  198.0 2.4 fusion.70
  202.2 38.6 %all-gather = f32[512,4,5]{2,1,0:T(4,128)S(1)} all-gather(f32[64,4,5]{2,1,0:T(4,128)S(1)} %get-tuple-element.232), channel_id=2, replica_groups=mesh['gx'=4,'gy'=8] {'gy'}, dimensions={0}, use_global_device_ids=true | all-gather | bytes 46080 | tf_op jit(solution)/shard_map/all_gather | solution.py:18
  240.9 35.2 %all-gather.1 = f32[512,4,5]{2,1,0:T(4,128)S(1)} all-gather(f32[64,4,5]{2,1,0:T(4,128)S(1)} %get-tuple-element.233), channel_id=3, replica_groups=mesh['gx'=4,'gy'=8] {'gy'}, dimensions={0}, use_global_device_ids=true | all-gather | bytes 46080 | tf_op jit(solution)/shard_map/all_gather | solution.py:18
  282.6 27.2 %all-gather.7.cloned.1.call-done = f32[512,4,5,128]{3,0,2,1:T(8,128)} async-done(((f32[64,4,5,128]{3,0,2,1:T(8,128)}), f32[512,4,5,128]{3,0,2,1:T(8,128)}) %all-gather.7.cloned.1.call-update) | async-done | bytes 5242896 | tf_op jit(solution)/shard_map/all_gather | solution.py:18
  311.4 20.6 while.34
  336.7 19.3 psum.7
  356.3 2.1 scatter_custom_fusion
  358.7 12.1 all_to_all.10
  370.8 16.6 fusion.23
  388.2 1891.7 %all-gather.9.cloned.1.call-done = f32[32,16,12,3072]{3,2,0,1:T(8,128)} async-done(((f32[4,16,12,3072]{3,2,0,1:T(8,128)}), f32[32,16,12,3072]{3,2,0,1:T(8,128)}) %all-gather.9.cloned.1.call-update) | async-done | bytes 75497488 | tf_op jit(solution)/shard_map/all_gather | solution.py:104
  2279.8 36.1 %reduce_sum.60 = f32[4,16,12,3072]{3,2,0,1:T(8,128)} reduce(f32[8,4,16,12,3072]{4,3,1,0,2:T(8,128)} %bitcast.12, f32[]{:T(128)} %constant.103.clone.1), dimensions={0}, to_apply=%region_14.15 | reduce | flops 16515072 | bytes 84934656 | tf_op jit(solution)/shard_map/reduce_sum | solution.py:104
  2316.0 11.6 fusion.34
  2328.8 3.5 all-to-all-start.1
  2332.5 9.2 all-to-all-done.1
  2342.2 2.1 gather_fusion.2
  (263 shorter events, 84.0 us)
Async XLA Ops:
  6.5 329.4 %copy-start = (bf16[2560,320]{0,1:T(8,128)(2,1)S(1)}, bf16[2560,320]{0,1:T(8,128)(2,1)}, u32[]{:S(2)}) copy-start(bf16[2560,320]{0,1:T(8,128)(2,1)} %param.21) | copy-start | bytes 4915204
  6.5 303.3 %all-gather.7.cloned.1.call-start = ((), (), s32[]{:S(2)}) async-start(), calls=%async_computation.2 | async-start | bytes 5898240 | tf_op jit(solution)/shard_map/all_gather | solution.py:18
  13.6 7.5 copy-start.7
  13.6 8.8 copy-start.2
  22.4 179.4 %copy-start.8 = (s32[256,6]{0,1:T(8,128)S(1)}, s32[256,6]{0,1:T(8,128)}, u32[]{:S(2)}) copy-start(s32[256,6]{0,1:T(8,128)} %param.24) | copy-start | bytes 18436
  200.4 78.9 %copy-start.4 = (bf16[64,1024]{1,0:T(8,128)(2,1)S(1)}, bf16[64,1024]{1,0:T(8,128)(2,1)}, u32[]{:S(2)}) copy-start(bf16[64,1024]{1,0:T(8,128)(2,1)} %param.17) | copy-start | bytes 393220
  200.5 80.5 %copy-start.9 = (bf16[320]{0:T(512)(128)(2,1)S(1)}, bf16[320]{0:T(512)(128)(2,1)}, u32[]{:S(2)}) copy-start(bf16[320]{0:T(512)(128)(2,1)} %param.23) | copy-start | bytes 1924
  200.5 2079.4 %all-gather.9.cloned.1.call-start = ((), (), s32[]{:S(2)}) async-start(), calls=%async_computation.3 | async-start | bytes 113246208 | tf_op jit(solution)/shard_map/all_gather | solution.py:104
  276.2 1.0 copy-start.3
  311.4 24.6 %copy-start.5 = (bf16[64,320]{1,0:T(8,128)(2,1)S(1)}, bf16[64,320]{1,0:T(8,128)(2,1)}, u32[]{:S(2)}) copy-start(bf16[64,320]{1,0:T(8,128)(2,1)} %param.22) | copy-start | bytes 122884
  387.4 0.7 copy-start.6
  2327.6 17.8 copy-start.1
  2328.8 13.0 all-to-all-start.1
Sparse Core Ops, SparseCore 0:
  200.6 109.1 all-gather.6
  387.6 1892.2 all-gather.8
